TPU v7x, 512 devices: a whole 4x4x16 slice. The times are simulated.
512 devices in a mesh: ctx: 64 (over y, z), exp: 8 (over x, core).
Axes of the slice: x: 4, y: 4, z: 16, core: 2. Of those that a mesh axis runs over, the one named last changes fastest.
Arguments:
- queries: bfloat16 [8192, 4096], P('ctx', 'exp'), may hold values from -24 to 24
- key_rows: bfloat16 [8192, 1024], P('ctx', 'exp'), may hold values from -24 to 24
- mixer_input: bfloat16 [8192, 8192], P('ctx', 'exp'), may hold values from -32 to 32
- gate_input: bfloat16 [8192, 8192], P('ctx', 'exp'), may hold values from -6 to 6
- write_proj: bfloat16 [8192, 128], P('ctx'), may hold values from -0.5 to 0.5
- read_proj: bfloat16 [8192, 128], P('ctx'), may hold values from -0.5 to 0.5
- step_size: float32 [8192, 128], P('ctx', 'exp'), may hold values from 0.5 to 2
- log_decay: float32 [8192, 128], P('ctx', 'exp'), may hold values from -1.7 to 0
- skip_gain: float32 [128], P('exp'), may hold values from 0.5 to 2
- norm_gain: float32 [8192], P('exp'), may hold values from 0.1 to 1.9
- value_weight: bfloat16 [8192, 1024], P('exp'), may hold values from -0.09375 to 0.09375
Outputs:
- attention_out: bfloat16 [8192, 4096], P('ctx', 'exp')
- mixer_out: bfloat16 [8192, 8192], P('ctx', 'exp')
All inputs are finite; a program needn't handle non-finite values.
Results may differ from a plain program's by a relative error of at most 0.018.
Values may be sent and summed in bfloat16 or wider, within the bound.
A program may use at most 64 MiB of HBM per device.

v0:
```python
import jax
import jax.numpy as jnp
from jax import lax
from jax.sharding import PartitionSpec as P

QUERY_HEADS = 32
KEY_HEADS = 8
HEAD_DIM = 128
MIXER_HEADS = 128
MIXER_CHANNELS = 64
STATE_SIZE = 128
BLOCK_LEN = 128
rope_base = 10000.0
rope_stretch = 4.0
norm_eps = 1e-05
floor_score = -1e30


def entering(x, axis, join, neutral):
    place = lax.axis_index(axis)
    gathered = jax.tree.map(
        lambda a, kind: lax.all_gather(a.astype(kind), axis), x, (jnp.bfloat16, jnp.bfloat16)
    )
    state = jax.tree.map(lambda a, e: jnp.zeros_like(a) + jnp.asarray(e, a.dtype), x, neutral)

    def one(lap, state):
        return join(
            state,
            jax.tree.map(
                lambda a, own: lax.dynamic_index_in_dim(a, lap, 0, False).astype(own.dtype),
                gathered,
                x,
            ),
        )

    return lax.fori_loop(0, place, one, state)


def rotate(vectors, positions, head_width):
    halfway = head_width // 2
    frequency = rope_base ** (-(2.0 * jnp.arange(halfway, dtype=jnp.float32)) / head_width)
    angles = (positions.astype(jnp.float32) / rope_stretch)[:, None] * frequency[None, :]
    cosine = jnp.cos(angles)[:, None, :]
    sine_part = jnp.sin(angles)[:, None, :]
    front_half = vectors[..., :halfway].astype(jnp.float32)
    back_half = vectors[..., halfway:].astype(jnp.float32)
    turned = jnp.concatenate(
        [front_half * cosine - back_half * sine_part, back_half * cosine + front_half * sine_part],
        axis=-1,
    )
    return turned.astype(jnp.bfloat16)


def attend_update(
    running, query_group, query_pos, key_block, value_block, key_pos, group_low, group_high
):
    running_max, running_sum, running_out = running
    scores = jnp.einsum(
        "cgtd,scd->cgts", query_group, key_block, preferred_element_type=jnp.float32
    ) * HEAD_DIM ** (-0.5)
    allowed = key_pos[None, :] <= query_pos[:, None]
    masked = jnp.where(allowed, scores, floor_score)
    new_max = jnp.maximum(running_max, jnp.max(masked, axis=-1))
    weights = jnp.where(allowed, jnp.exp(masked - new_max[..., None]), 0.0)
    factor = jnp.exp(running_max - new_max)
    new_sum = running_sum * factor + jnp.sum(weights, axis=-1)
    update = jnp.einsum(
        "cgts,scd->cgtd",
        weights.astype(jnp.bfloat16),
        value_block,
        preferred_element_type=jnp.float32,
    )
    new_out = running_out * factor[..., None] + update
    return (
        running_max.at[:, :, group_low:group_high].set(new_max),
        running_sum.at[:, :, group_low:group_high].set(new_sum),
        running_out.at[:, :, group_low:group_high].set(new_out),
    )


def attention(queries, key_rows, value_rows):
    row_count = queries.shape[0]
    kv_local = key_rows.shape[1] // HEAD_DIM
    group_size = QUERY_HEADS // KEY_HEADS
    shard_index = lax.axis_index("ctx")
    local_pos = jnp.arange(row_count, dtype=jnp.int32)
    groups = ((0, row_count),)
    query_pos = shard_index * row_count + local_pos
    turned_q = rotate(
        queries.reshape(row_count, kv_local * group_size, HEAD_DIM), query_pos, HEAD_DIM
    )
    query_mat = jnp.transpose(
        turned_q.reshape(row_count, kv_local, group_size, HEAD_DIM), (1, 2, 0, 3)
    )
    turned_k = rotate(key_rows.reshape(row_count, kv_local, HEAD_DIM), query_pos, HEAD_DIM)
    value_mat = value_rows.reshape(row_count, kv_local, HEAD_DIM)
    initial = (
        jnp.full((kv_local, group_size, row_count), floor_score, jnp.float32),
        jnp.zeros((kv_local, group_size, row_count), jnp.float32),
        jnp.zeros((kv_local, group_size, row_count, HEAD_DIM), jnp.float32),
    )
    piece_keys = lax.all_gather(turned_k, "ctx", axis=0, tiled=True)
    piece_values = lax.all_gather(value_mat, "ctx", axis=0, tiled=True)
    piece_rows = piece_keys.shape[0]
    piece_pos = jnp.arange(piece_rows, dtype=jnp.int32)

    def key_step(step_index, current):
        offset = step_index * row_count
        block_keys = lax.dynamic_slice_in_dim(piece_keys, offset, row_count, 0)
        block_values = lax.dynamic_slice_in_dim(piece_values, offset, row_count, 0)
        block_pos = lax.dynamic_slice_in_dim(piece_pos, offset, row_count, 0)
        group_low, group_high = groups[0]
        group_pos = query_pos

        def group_update(state_in, group_low=group_low, group_high=group_high, group_pos=group_pos):
            return attend_update(
                state_in,
                query_mat,
                group_pos,
                block_keys,
                block_values,
                block_pos,
                group_low,
                group_high,
            )

        def unchanged(state_in):
            return state_in

        needed = jnp.min(block_pos) <= jnp.max(group_pos)
        current = lax.cond(needed, group_update, unchanged, current)
        return current

    result = lax.fori_loop(0, piece_rows // row_count, key_step, initial)
    running_max, running_sum, running_out = result
    merged = running_out / running_sum[..., None]
    finished = (
        jnp.transpose(merged, (2, 0, 1, 3))
        .reshape(row_count, kv_local * group_size * HEAD_DIM)
        .astype(jnp.bfloat16)
    )
    return finished


def chain_join(earlier, later):
    return (earlier[0] + later[0], jnp.exp(later[0])[:, None, None] * earlier[1] + later[1])


def mixer_block(
    mixer_input, gate_input, write_proj, read_proj, step_size, log_decay, skip_gain, norm_gain
):
    row_count = mixer_input.shape[0]
    head_count = step_size.shape[1]
    block_count = row_count // BLOCK_LEN
    shaped_x = mixer_input.reshape(block_count, BLOCK_LEN, head_count, MIXER_CHANNELS)
    causal = jnp.arange(BLOCK_LEN)[:, None] >= jnp.arange(BLOCK_LEN)[None, :]
    agg_state = jnp.zeros((head_count, MIXER_CHANNELS, STATE_SIZE), jnp.float32)
    block_x = shaped_x[0]
    block_read = read_proj
    cumul = jnp.cumsum(log_decay, axis=0)
    gram = jnp.einsum("tn,sn->ts", block_read, write_proj, preferred_element_type=jnp.float32)
    cumul_heads = cumul.T
    spread = cumul_heads[:, :, None] - cumul_heads[:, None, :]
    decay = jnp.where(causal[None], jnp.exp(jnp.where(causal[None], spread, 0.0)), 0.0)
    mixing = (decay * gram[None] * step_size.T[:, None, :]).astype(jnp.bfloat16)
    intra = jnp.einsum("hts,shp->thp", mixing, block_x, preferred_element_type=jnp.float32)
    ending = cumul[-1]
    weighted = (
        block_x.astype(jnp.float32) * (step_size * jnp.exp(ending[None, :] - cumul))[:, :, None]
    ).astype(jnp.bfloat16)
    local_state = jnp.einsum(
        "shp,sn->hpn", weighted, write_proj, preferred_element_type=jnp.float32
    )
    agg_state = jnp.exp(ending)[:, None, None] * agg_state + local_state
    agg_decay = ending
    saved = (intra, cumul, ending, local_state, block_read, block_x)
    incoming = entering(
        (agg_decay, agg_state),
        "ctx",
        chain_join,
        (
            jnp.zeros((head_count,), jnp.float32),
            jnp.zeros((head_count, MIXER_CHANNELS, STATE_SIZE), jnp.float32),
        ),
    )
    carried = incoming[1]
    intra, cumul, ending, local_state, block_read, block_x = saved
    inter = (
        jnp.einsum(
            "tn,hpn->thp", block_read.astype(jnp.float32), carried, precision=lax.Precision.HIGHEST
        )
        * jnp.exp(cumul)[:, :, None]
    )
    pieces_out = intra + inter + skip_gain[None, :, None] * block_x.astype(jnp.float32)
    gate_full = gate_input.reshape(row_count, head_count, MIXER_CHANNELS).astype(jnp.float32)
    gated = pieces_out * jax.nn.silu(gate_full)
    partial_square = jnp.sum(gated * gated, axis=(1, 2))
    total_square = lax.psum(partial_square, "exp")
    mean_square = total_square / (MIXER_HEADS * MIXER_CHANNELS)
    normed = (
        gated
        * lax.rsqrt(mean_square + norm_eps)[:, None, None]
        * norm_gain.reshape(head_count, MIXER_CHANNELS)
    )
    return normed.reshape(row_count, head_count * MIXER_CHANNELS).astype(jnp.bfloat16)


def on_device(
    queries,
    key_rows,
    mixer_input,
    gate_input,
    write_proj,
    read_proj,
    step_size,
    log_decay,
    skip_gain,
    norm_gain,
    value_weight,
):
    mixer_out = mixer_block(
        mixer_input, gate_input, write_proj, read_proj, step_size, log_decay, skip_gain, norm_gain
    )
    value_terms = jnp.dot(mixer_out, value_weight, preferred_element_type=jnp.float32)
    value_rows = lax.psum_scatter(
        value_terms.astype(jnp.bfloat16), "exp", scatter_dimension=1, tiled=True
    )
    attention_out = attention(queries, key_rows, value_rows)
    return (attention_out, mixer_out)


def solution(mesh):
    return jax.shard_map(
        on_device,
        mesh=mesh,
        in_specs=(
            P("ctx", "exp"),
            P("ctx", "exp"),
            P("ctx", "exp"),
            P("ctx", "exp"),
            P("ctx", None),
            P("ctx", None),
            P("ctx", "exp"),
            P("ctx", "exp"),
            P("exp"),
            P("exp"),
            P("exp", None),
        ),
        out_specs=(P("ctx", "exp"), P("ctx", "exp")),
        check_vma=False,
    )
```

profile of v0, /device:TPU:504, one launch (start us, length us, event | category | flops | bytes accessed | tf_op | source)
XLA Modules:
  0.0 883.1 jit_solution(17325050694433945698)
XLA Ops:
  12.2 70.4 %all-gather.2 = bf16[64,1,16]{2,1,0:T(2,128)(2,1)S(1)} all-gather(bf16[1,1,16]{2,1,0:T(2,128)(2,1)S(1)} %convert_bitcast_fusion), channel_id=1, replica_groups=mesh['ctx'=64,'exp'=8] {'ctx'}, dimensions={0}, use_global_device_ids=true | all-gather | bytes 2080 | tf_op jit(solution)/shard_map/all_gather | solution.py:22
  84.7 114.7 %all-gather.9.cloned.1.call-done = bf16[1024,64,128]{2,1,0:T(8,128)(2,1)} async-done(((bf16[16,64,128]{2,1,0:T(8,128)(2,1)}), bf16[1024,64,128]{2,1,0:T(8,128)(2,1)}) %all-gather.9.cloned.1.call-update) | async-done | bytes 16777232 | tf_op jit(solution)/shard_map/all_gather | solution.py:22
  199.5 73.2 %while.37 = (s32[]{:T(128)}, f32[16,64,128]{2,1,0:T(8,128)S(1)}, s32[]{:T(128)}, bf16[64,16]{1,0:T(8,128)(2,1)S(1)}, bf16[64,16,64,128]{3,2,1,0:T(8,128)(2,1)}, /*index=5*/s32[]{:T(128)}, s32[]{:T(128)}, s32[]{:T(128)}) while((s32[]{:T(128)}, f32[16,64,128]{2,1,0:T(8,128)S(1)}, s32[]{:T(128)}, bf16[64,16]{1,0:T(8,128)(2,1)S(1)}, ...), condition=%wide.region_2.3_spmd, body=%wide.region_1.2_spmd.sunk | while | flops 393237 | bytes 1311007 | solution.py:36
  272.6 2.3 multiply_reduce_fusion
  275.0 13.8 %psum.7 = f32[128]{0:T(128)S(1)} all-reduce(f32[128]{0:T(128)S(1)} %get-tuple-element.521), channel_id=1, replica_groups=mesh['ctx'=64,'exp'=8] {'exp'}, use_global_device_ids=true, to_apply=%region_4.5 | all-reduce | flops 128 | bytes 1024 | tf_op jit(solution)/shard_map/psum | solution.py:198
  292.4 29.7 %reduce-scatter.4.cloned.1.call-done = bf16[128,128]{1,0:T(8,128)(2,1)} async-done(((bf16[1024,128]{1,0:T(8,128)(2,1)}), bf16[128,128]{1,0:T(8,128)(2,1)}) %reduce-scatter.4.cloned.1.call-update) | async-done | bytes 32784
  324.8 132.9 %all-gather.7.cloned.1.call-done = bf16[8192,1,128]{0,2,1:T(8,128)(2,1)} async-done(((bf16[128,1,128]{0,2,1:T(8,128)(2,1)}), bf16[8192,1,128]{0,2,1:T(8,128)(2,1)}) %all-gather.7.cloned.1.call-update) | async-done | bytes 2097168 | tf_op jit(solution)/shard_map/all_gather | solution.py:102
  457.7 4.1 copy.67
  462.6 134.0 %all-gather.11.cloned.1.call-done = bf16[8192,128]{1,0:T(8,128)(2,1)} async-done(((bf16[128,128]{1,0:T(8,128)(2,1)}), bf16[8192,128]{1,0:T(8,128)(2,1)}) %all-gather.11.cloned.1.call-update) | async-done | bytes 2097168 | tf_op jit(solution)/shard_map/all_gather | solution.py:103
  596.7 278.9 %while.38 = (s32[]{:T(128)}, f32[1,4,128]{2,1,0:T(4,128)S(1)}, f32[1,4,128]{2,1,0:T(4,128)S(1)}, f32[1,4,128,128]{3,2,1,0:T(8,128)S(1)}, s32[8192]{0:T(1024)S(1)...) while((s32[]{:T(128)}, f32[1,4,128]{2,1,0:T(4,128)S(1)}, ...), condition=%wide.region_13.14_spmd.clone, body=%wide.region_7.0_spmd.clone.sunk | while | flops 34293512 | bytes 1610581 | solution.py:134
  598.8 2.2 conditional.3
  611.9 2.2 conditional.3
  620.6 2.2 conditional.3
  629.3 2.2 conditional.3
  638.0 2.2 conditional.3
  646.7 2.2 conditional.3
  655.4 2.2 conditional.3
  664.2 2.2 conditional.3
  672.9 2.2 conditional.3
  681.6 2.2 conditional.3
  690.3 2.2 conditional.3
  699.0 2.2 conditional.3
  707.7 2.2 conditional.3
  716.5 2.2 conditional.3
  (885 shorter events, 387.3 us)
Async XLA Ops:
  7.2 282.9 %copy-start = (bf16[1024,1024]{1,0:T(8,128)(2,1)S(1)}, bf16[1024,1024]{1,0:T(8,128)(2,1)}, u32[]{:S(2)}) copy-start(bf16[1024,1024]{1,0:T(8,128)(2,1)} %param.39) | copy-start | bytes 6291460
  7.2 76.1 %copy-start.6 = (f32[128,16]{0,1:T(8,128)S(1)}, f32[128,16]{0,1:T(8,128)}, u32[]{:S(2)}) copy-start(f32[128,16]{0,1:T(8,128)} %param.35) | copy-start | bytes 24580
  7.2 76.0 %copy-start.3 = (bf16[128,128]{1,0:T(8,128)(2,1)S(1)}, bf16[128,128]{1,0:T(8,128)(2,1)}, u32[]{:S(2)}) copy-start(bf16[128,128]{1,0:T(8,128)(2,1)} %param.33) | copy-start | bytes 98308
  7.2 75.6 %copy-start.1 = (bf16[128,1024]{1,0:T(8,128)(2,1)S(1)}, bf16[128,1024]{1,0:T(8,128)(2,1)}, u32[]{:S(2)}) copy-start(bf16[128,1024]{1,0:T(8,128)(2,1)} %param.32) | copy-start | bytes 786436
  7.2 75.7 %copy-start.7 = (f32[1024]{0:T(1024)S(1)}, f32[1024]{0:T(1024)}, u32[]{:S(2)}) copy-start(f32[1024]{0:T(1024)} %param.38) | copy-start | bytes 12292
  7.2 75.8 %copy-start.4 = (bf16[128,128]{1,0:T(8,128)(2,1)S(1)}, bf16[128,128]{1,0:T(8,128)(2,1)}, u32[]{:S(2)}) copy-start(bf16[128,128]{1,0:T(8,128)(2,1)} %param.30) | copy-start | bytes 98308
  7.2 76.0 %copy-start.5 = (bf16[128,128]{1,0:T(8,128)(2,1)S(1)}, bf16[128,128]{1,0:T(8,128)(2,1)}, u32[]{:S(2)}) copy-start(bf16[128,128]{1,0:T(8,128)(2,1)} %param.34) | copy-start | bytes 98308
  7.2 192.2 %all-gather.9.cloned.1.call-start = ((), (), s32[]{:S(2)}) async-start(), calls=%async_computation.2 | async-start | bytes 17039360 | tf_op jit(solution)/shard_map/all_gather | solution.py:22
  12.2 309.9 %reduce-scatter.4.cloned.1.call-start = ((), (), s32[]{:S(2)}) async-start(), calls=%async_computation.4 | async-start | bytes 294912
  199.5 73.2 %copy-start.8 = (f32[16]{0:T(128)S(1)}, f32[16]{0:T(128)}, u32[]{:S(2)}) copy-start(f32[16]{0:T(128)} %param.37) | copy-start | bytes 196
  288.8 35.5 %copy-start.2 = (bf16[128,512]{1,0:T(8,128)(2,1)S(1)}, bf16[128,512]{1,0:T(8,128)(2,1)}, u32[]{:S(2)}) copy-start(bf16[128,512]{1,0:T(8,128)(2,1)} %param.29) | copy-start | bytes 393220
  291.4 166.3 %all-gather.7.cloned.1.call-start = ((), (), s32[]{:S(2)}) async-start(), calls=%async_computation.1 | async-start | bytes 2129920 | tf_op jit(solution)/shard_map/all_gather | solution.py:102
  292.4 304.3 %all-gather.11.cloned.1.call-start = ((), (), s32[]{:S(2)}) async-start(), calls=%async_computation.3 | async-start | bytes 2129920 | tf_op jit(solution)/shard_map/all_gather | solution.py:103
Sparse Core Ops, SparseCore 0:
  12.3 187.0 all-gather.8
  291.6 30.4 reduce-scatter.3
  325.6 132.0 all-gather.6
  460.5 136.0 all-gather.10
where the time goes:
time: 895 us; the launch traced here: 883 us
  waiting for transfers between devices  411 us (46%)
  other arithmetic  135 us (15%)
  matrix products  134 us (15%)
  loops' own time  91.8 us (10%)
  blocking collectives  84.2 us (9%)
  between operations  14 us (2%)
  local copies, waits for them, and re-layouts  12.1 us (1%)
    all_gather x1, waiting for transfers between devices, attention(): piece_values = lax.all_gather(value_mat, 'ctx', axis=0, tiled=True)  134 us
    all_gather x1, waiting for transfers between devices, attention(): piece_keys = lax.all_gather(turned_k, 'ctx', axis=0, tiled=True)  133 us
    all_gather x1, waiting for transfers between devices, entering(): lax.all_gather(a.astype(kind), axis)  115 us
    another operation x1, loops' own time, attention(): result = lax.fori_loop(0, piece_rows // row_count, key_step, initial)  86 us
    all_gather x1, blocking collectives, entering(): lax.all_gather(a.astype(kind), axis)  70.4 us
    add x63, other arithmetic, chain_join(): jnp.exp(later[0])[:, None, None] * earlier[1] + later[1]  70 us
    dot_general x64, matrix products, attend_update(): jnp.einsum('cgts,scd->cgtd', weights.astype(jnp.bfloat16), value_block, p...  66.4 us
    dot_general x64, matrix products, attend_update(): jnp.einsum('cgtd,scd->cgts', query_group, key_block, preferred_element_ty...  61.9 us
  transfers between devices with their start and end apart: 4, of which 4 were waited for; matrix products, arithmetic and copies ran while one was open for 1% of the time, Pallas kernels for 0%

commit v1 on v0

--- a/solution.py
+++ b/solution.py
@@ -99,7 +99,9 @@
         jnp.zeros((kv_local, group_size, row_count), jnp.float32),
         jnp.zeros((kv_local, group_size, row_count, HEAD_DIM), jnp.float32),
     )
-    piece_keys = lax.all_gather(turned_k, "ctx", axis=0, tiled=True)
+    piece_keys = jnp.concatenate(
+        lax.all_to_all(jnp.stack([turned_k] * lax.axis_size("ctx")), "ctx", 0, 0), axis=0
+    )
     piece_values = lax.all_gather(value_mat, "ctx", axis=0, tiled=True)
     piece_rows = piece_keys.shape[0]
     piece_pos = jnp.arange(piece_rows, dtype=jnp.int32)

time: 895 us -> 809 us (0.904)
  waiting for transfers between devices: 411 us -> 220 us
  blocking collectives: 84.2 us -> 192 us
  starting transfers between devices: 0.16 us -> 12.4 us
    all_gather x1 -> x0, waiting for transfers between devices: 133 us -> none  [attention(): piece_keys = lax.all_gather(turned_k, 'ctx', axis=0, tiled=True)]
    all_gather x1, blocking collectives: 70.4 us -> 178 us  [entering(): lax.all_gather(a.astype(kind), axis)]
    all_gather x1, waiting for transfers between devices: 115 us -> 52.3 us  [entering(): lax.all_gather(a.astype(kind), axis)]
    all_to_all x0 -> x1, starting transfers between devices: none -> 12.3 us  [attention(): lax.all_to_all(jnp.stack([turned_k] * lax.axis_size('ctx')), 'ctx', 0, 0)]
    unnamed x5 -> x4, waiting for transfers between devices: 29.7 us -> 30.6 us
  transfers between devices with their start and end apart: 4 -> 4, of which waited for: 4 -> 3; matrix products, arithmetic and copies ran while one was open for 1% -> 11% of each run, Pallas kernels for 0% -> 0%
where the time goes in v1:
time: 809 us; the launch traced here: 797 us
  waiting for transfers between devices  220 us (27%)
  blocking collectives  192 us (24%)
  matrix products  134 us (17%)
  other arithmetic  130 us (16%)
  loops' own time  85.1 us (11%)
  between operations  14 us (2%)
  starting transfers between devices  12.4 us (2%)
  local copies, waits for them, and re-layouts  9.7 us (1%)
    all_gather x1, blocking collectives, entering(): lax.all_gather(a.astype(kind), axis)  178 us
    all_gather x1, waiting for transfers between devices, attention(): piece_values = lax.all_gather(value_mat, 'ctx', axis=0, tiled=True)  137 us
    another operation x1, loops' own time, attention(): result = lax.fori_loop(0, piece_rows // row_count, key_step, initial)  79.3 us
    add x63, other arithmetic, chain_join(): jnp.exp(later[0])[:, None, None] * earlier[1] + later[1]  70 us
    dot_general x64, matrix products, attend_update(): jnp.einsum('cgts,scd->cgtd', weights.astype(jnp.bfloat16), value_block, p...  66.4 us
    dot_general x64, matrix products, attend_update(): jnp.einsum('cgtd,scd->cgts', query_group, key_block, preferred_element_ty...  61.8 us
    all_gather x1, waiting for transfers between devices, entering(): lax.all_gather(a.astype(kind), axis)  52.3 us
    reduce_min x64, other arithmetic, key_step(): needed = jnp.min(block_pos) <= jnp.max(group_pos)  43.5 us
  transfers between devices with their start and end apart: 4, of which 3 were waited for; matrix products, arithmetic and copies ran while one was open for 11% of the time, Pallas kernels for 0%

profile of v1, /device:TPU:504, one launch (start us, length us, event | category | flops | bytes accessed | tf_op | source)
XLA Modules:
  0.0 796.9 jit_solution(4622335085679747239)
XLA Ops:
  15.2 12.3 %all-to-all-start = ((bf16[64,128,1,128]{3,1,2,0:T(8,128)(2,1)}), bf16[64,128,1,128]{3,1,2,0:T(8,128)(2,1)}, u32[]{:S(2)}, u32[]{:S(2)}) async-start(bf16[64,128,1,128]{3,1,2,0:T(8,128)(2,1)} %stack.2), calls=%async_computation | async-start | bytes 4194304 | tf_op jit(solution)/shard_map/all_to_all | solution.py:103
  27.6 177.6 %all-gather.2 = bf16[64,1,16]{2,1,0:T(2,128)(2,1)S(1)} all-gather(bf16[1,1,16]{2,1,0:T(2,128)(2,1)S(1)} %convert_bitcast_fusion), channel_id=1, replica_groups=mesh['ctx'=64,'exp'=8] {'ctx'}, dimensions={0}, use_global_device_ids=true | all-gather | bytes 2080 | tf_op jit(solution)/shard_map/all_gather | solution.py:22
  207.1 52.3 %all-gather.6.cloned.1.call-done = bf16[1024,64,128]{2,1,0:T(8,128)(2,1)} async-done(((bf16[16,64,128]{2,1,0:T(8,128)(2,1)}), bf16[1024,64,128]{2,1,0:T(8,128)(2,1)}) %all-gather.6.cloned.1.call-update) | async-done | bytes 16777232 | tf_op jit(solution)/shard_map/all_gather | solution.py:22
  259.5 73.1 %while.37 = (s32[]{:T(128)}, f32[16,64,128]{2,1,0:T(8,128)S(1)}, s32[]{:T(128)}, bf16[64,16]{1,0:T(8,128)(2,1)S(1)}, bf16[64,16,64,128]{3,2,1,0:T(8,128)(2,1)}, /*index=5*/s32[]{:T(128)}, s32[]{:T(128)}, s32[]{:T(128)}) while((s32[]{:T(128)}, f32[16,64,128]{2,1,0:T(8,128)S(1)}, s32[]{:T(128)}, bf16[64,16]{1,0:T(8,128)(2,1)S(1)}, ...), condition=%wide.region_2.3_spmd, body=%wide.region_1.2_spmd.sunk | while | flops 393237 | bytes 1311007 | solution.py:36
  332.6 2.3 multiply_reduce_fusion
  335.0 14.1 %psum.7 = f32[128]{0:T(128)S(1)} all-reduce(f32[128]{0:T(128)S(1)} %get-tuple-element.504), channel_id=1, replica_groups=mesh['ctx'=64,'exp'=8] {'exp'}, use_global_device_ids=true, to_apply=%region_4.5 | all-reduce | flops 128 | bytes 1024 | tf_op jit(solution)/shard_map/psum | solution.py:200
  351.8 30.6 %reduce-scatter.4.cloned.1.call-done = bf16[128,128]{1,0:T(8,128)(2,1)} async-done(((bf16[1024,128]{1,0:T(8,128)(2,1)}), bf16[128,128]{1,0:T(8,128)(2,1)}) %reduce-scatter.4.cloned.1.call-update) | async-done | bytes 32784
  385.9 137.2 %all-gather.8.cloned.1.call-done = bf16[8192,128]{1,0:T(8,128)(2,1)} async-done(((bf16[128,128]{1,0:T(8,128)(2,1)}), bf16[8192,128]{1,0:T(8,128)(2,1)}) %all-gather.8.cloned.1.call-update) | async-done | bytes 2097168 | tf_op jit(solution)/shard_map/all_gather | solution.py:105
  523.2 266.2 %while.38 = (s32[]{:T(128)}, f32[1,4,128]{2,1,0:T(4,128)S(1)}, f32[1,4,128]{2,1,0:T(4,128)S(1)}, f32[1,4,128,128]{3,2,1,0:T(8,128)S(1)}, s32[8192]{0:T(1024)S(1)...) while((s32[]{:T(128)}, f32[1,4,128]{2,1,0:T(4,128)S(1)}, ...), condition=%wide.region_13.14_spmd.clone, body=%wide.region_7.0_spmd.clone.sunk | while | flops 34293512 | bytes 1610581 | solution.py:136
  525.1 2.2 conditional.3
  529.3 2.2 conditional.3
  533.4 2.2 conditional.3
  537.6 2.2 conditional.3
  541.7 2.2 conditional.3
  545.9 2.2 conditional.3
  550.1 2.2 conditional.3
  554.2 2.2 conditional.3
  558.4 2.2 conditional.3
  562.5 2.2 conditional.3
  566.7 2.2 conditional.3
  570.9 2.2 conditional.3
  575.0 2.2 conditional.3
  579.2 2.2 conditional.3
  583.3 2.2 conditional.3
  (881 shorter events, 381.1 us)
Async XLA Ops:
  7.2 343.2 %copy-start = (bf16[1024,1024]{1,0:T(8,128)(2,1)S(1)}, bf16[1024,1024]{1,0:T(8,128)(2,1)}, u32[]{:S(2)}) copy-start(bf16[1024,1024]{1,0:T(8,128)(2,1)} %param.39) | copy-start | bytes 6291460
  7.2 252.2 %all-gather.6.cloned.1.call-start = ((), (), s32[]{:S(2)}) async-start(), calls=%async_computation.2 | async-start | bytes 17039360 | tf_op jit(solution)/shard_map/all_gather | solution.py:22
  15.2 190.1 %copy-start.1 = (bf16[128,1024]{1,0:T(8,128)(2,1)S(1)}, bf16[128,1024]{1,0:T(8,128)(2,1)}, u32[]{:S(2)}) copy-start(bf16[128,1024]{1,0:T(8,128)(2,1)} %param.32) | copy-start | bytes 786436
  15.2 190.3 %copy-start.6 = (f32[1024]{0:T(1024)S(1)}, f32[1024]{0:T(1024)}, u32[]{:S(2)}) copy-start(f32[1024]{0:T(1024)} %param.38) | copy-start | bytes 12292
  15.2 190.4 %copy-start.3 = (bf16[128,128]{1,0:T(8,128)(2,1)S(1)}, bf16[128,128]{1,0:T(8,128)(2,1)}, u32[]{:S(2)}) copy-start(bf16[128,128]{1,0:T(8,128)(2,1)} %param.33) | copy-start | bytes 98308
  15.2 190.4 %copy-start.4 = (bf16[128,128]{1,0:T(8,128)(2,1)S(1)}, bf16[128,128]{1,0:T(8,128)(2,1)}, u32[]{:S(2)}) copy-start(bf16[128,128]{1,0:T(8,128)(2,1)} %param.34) | copy-start | bytes 98308
  15.2 190.5 %copy-start.5 = (f32[128,16]{0,1:T(8,128)S(1)}, f32[128,16]{0,1:T(8,128)}, u32[]{:S(2)}) copy-start(f32[128,16]{0,1:T(8,128)} %param.35) | copy-start | bytes 24580
  15.2 370.7 %all-to-all-start = ((bf16[64,128,1,128]{3,1,2,0:T(8,128)(2,1)}), bf16[64,128,1,128]{3,1,2,0:T(8,128)(2,1)}, u32[]{:S(2)}, u32[]{:S(2)}) async-start(bf16[64,128,1,128]{3,1,2,0:T(8,128)(2,1)} %stack.2), calls=%async_computation | async-start | bytes 4194304 | tf_op jit(solution)/shard_map/all_to_all | solution.py:103
  27.5 354.8 %reduce-scatter.4.cloned.1.call-start = ((), (), s32[]{:S(2)}) async-start(), calls=%async_computation.4 | async-start | bytes 294912
  259.5 73.1 %copy-start.7 = (f32[16]{0:T(128)S(1)}, f32[16]{0:T(128)}, u32[]{:S(2)}) copy-start(f32[16]{0:T(128)} %param.37) | copy-start | bytes 196
  349.1 35.5 %copy-start.2 = (bf16[128,512]{1,0:T(8,128)(2,1)S(1)}, bf16[128,512]{1,0:T(8,128)(2,1)}, u32[]{:S(2)}) copy-start(bf16[128,512]{1,0:T(8,128)(2,1)} %param.29) | copy-start | bytes 393220
  351.7 171.4 %all-gather.8.cloned.1.call-start = ((), (), s32[]{:S(2)}) async-start(), calls=%async_computation.3 | async-start | bytes 2129920 | tf_op jit(solution)/shard_map/all_gather | solution.py:105
Sparse Core Ops, SparseCore 0:
  12.2 247.1 all-gather.5
  351.8 30.4 reduce-scatter.3
  385.9 137.2 all-gather.7
